TPU v7x, 32 devices: a whole 2x2x4 slice. The times are simulated.
32 devices in a mesh: region: 8 (over z, core), state: 4 (over y, x).
Axes of the slice: x: 2, y: 2, z: 4, core: 2. Of those that a mesh axis runs over, the one named last changes fastest.
Arguments:
- state_anom: float32 [8, 16, 256, 512], P('region', 'state'), may hold values from -6 to 6
- obs_anom: float32 [8, 256, 512], P('region', 'state'), may hold values from -6 to 6
- obs_weight: float32 [8, 256, 512], P('region', 'state'), may hold values from -6 to 6
- obs_cell: int32 [8, 256], P('region', 'state'), may hold values from 0 to 255, as said below
- sector_of: int32 [8], replicated, may hold values from 0 to 7, as said below
Outputs:
- increment: float32 [8, 16, 256, 512], P('region', 'state')
Inputs may be any that keep to these rules, and one draw needn't show every extreme that they name: `obs_cell`: each entry is lon * 8 + lat with lon in 0..31 and lat in 0..7. Within each aligned block of 64 entries along the observation dimension the entries do not decrease; in each such block between 8 and 16 entries have lon < 8, and between 8 and 16 have lon >= 24; the bound 16 is reached on both sides in every draw. `sector_of`: A permutation: every region holds a different sector.
All inputs are finite; a program needn't handle non-finite values.
Results may differ from a plain program's by a relative error of at most 0.0003.
Values sent between devices are 32-bit elements; how exact they have to be, the bound alone decides.
No kernel may reach another device: no remote copies, remote signals or barrier semaphores. Data moves between devices by JAX's collectives and lax.ppermute only.
A program may use at most 64 MiB of HBM per device.

v0:
```python
import jax
import jax.numpy as jnp
from jax import lax
from jax.sharding import PartitionSpec as P

SECT_W = 32
LAT = 8
HALF = 4
CAP = 16
COLS = 256


def gaspari(scaled):
    inside = scaled * scaled * (scaled * (scaled * (0.5 - 0.25 * scaled) + 0.625) - 5.0 / 3.0) + 1.0
    floored = jnp.maximum(scaled, 1.0)
    outside = (
        scaled * (scaled * (scaled * (scaled * (scaled / 12.0 - 0.5) + 0.625) + 5.0 / 3.0) - 5.0)
        + 4.0
        - 2.0 / (3.0 * floored)
    )
    return jnp.where(scaled <= 1.0, inside, jnp.where(scaled < 2.0, outside, 0.0))


def taper_tile(state_cells, obs_cells, lon_span):
    state_lon = state_cells // LAT
    state_lat = state_cells % LAT
    obs_lon = obs_cells // LAT
    obs_lat = obs_cells % LAT
    lon_gap = state_lon[:, None] - obs_lon[None, :]
    lon_gap = (lon_gap + lon_span + lon_span // 2) % lon_span - lon_span // 2
    lat_gap = state_lat[:, None] - obs_lat[None, :]
    scaled = jnp.sqrt((lon_gap * lon_gap + lat_gap * lat_gap).astype(jnp.float32)) / HALF
    return gaspari(scaled)


def add_block(flat_state, state_cells, pieces, lon_span):
    piece_anom, piece_weight, piece_cells = pieces
    covar = jnp.einsum("rm,pm->rp", flat_state, piece_anom, precision=lax.Precision.HIGHEST)
    columns = state_cells.shape[0]
    levels_here = flat_state.shape[0] // columns
    tile = taper_tile(state_cells, piece_cells, lon_span) / (flat_state.shape[1] - 1)
    covar = (covar.reshape(levels_here, columns, -1) * tile[None]).reshape(flat_state.shape[0], -1)
    return jnp.dot(covar, piece_weight, precision=lax.Precision.HIGHEST)


def on_device(state_anom, obs_anom, obs_weight, obs_cell, sector_of):
    regions = lax.axis_size("region")
    lon_span = regions * SECT_W
    region_ids = jnp.arange(regions, dtype=jnp.int32)
    my_region = lax.axis_index("region")
    my_sector = jnp.sum(jnp.where(region_ids == my_region, sector_of, 0))
    left_region = jnp.sum(
        jnp.where(sector_of == (my_sector + regions - 1) % regions, region_ids, 0)
    )
    right_region = jnp.sum(jnp.where(sector_of == (my_sector + 1) % regions, region_ids, 0))
    own_anom = obs_anom[0]
    own_weight = obs_weight[0]
    own_cells = obs_cell[0] + my_sector * (SECT_W * LAT)
    count = own_anom.shape[0]
    low_set = (own_anom[:CAP], own_weight[:CAP], own_cells[:CAP])
    high_set = (own_anom[count - CAP :], own_weight[count - CAP :], own_cells[count - CAP :])
    to_left = region_ids == left_region
    to_right = region_ids == right_region

    def place(first, second):
        shaped = (regions,) + (1,) * first.ndim
        return jnp.where(to_left.reshape(shaped), first[None], 0) + jnp.where(
            to_right.reshape(shaped), second[None], 0
        )

    slotted = (
        lax.all_to_all(
            place(low_set[0], high_set[0]), "region", split_axis=0, concat_axis=0, tiled=True
        ),
        lax.all_to_all(
            place(low_set[1], high_set[1]), "region", split_axis=0, concat_axis=0, tiled=True
        ),
        lax.all_to_all(
            place(low_set[2], high_set[2]), "region", split_axis=0, concat_axis=0, tiled=True
        ),
    )
    from_left = tuple(
        (lax.dynamic_index_in_dim(pieces, left_region, 0, keepdims=False) for pieces in slotted)
    )
    from_right = tuple(
        (lax.dynamic_index_in_dim(pieces, right_region, 0, keepdims=False) for pieces in slotted)
    )
    halo_set = tuple(
        (
            jnp.concatenate([left_part, right_part], axis=0)
            for left_part, right_part in zip(from_left, from_right)
        )
    )
    flat_state = state_anom[0].reshape(-1, state_anom.shape[-1])
    state_cells = my_sector * (SECT_W * LAT) + jnp.arange(COLS, dtype=jnp.int32)
    joined = tuple(
        (
            jnp.concatenate([own_part, halo_part], axis=0)
            for own_part, halo_part in zip((own_anom, own_weight, own_cells), halo_set)
        )
    )
    total = add_block(
        flat_state,
        state_cells,
        (
            lax.all_gather(joined[0], "state", axis=0, tiled=True),
            lax.all_gather(joined[1], "state", axis=0, tiled=True),
            lax.all_gather(joined[2], "state", axis=0, tiled=True),
        ),
        lon_span,
    )
    return total.reshape(state_anom.shape)


def solution(mesh):
    in_specs = (
        P("region", "state", None, None),
        P("region", "state", None),
        P("region", "state", None),
        P("region", "state"),
        P(),
    )
    out_specs = P("region", "state", None, None)
    return jax.shard_map(
        on_device, mesh=mesh, in_specs=in_specs, out_specs=out_specs, check_vma=False
    )
```

profile of v0, /device:TPU:0, one launch (start us, length us, event | category | flops | bytes accessed | tf_op | source)
XLA Modules:
  0.0 79.8 jit_solution(260493578877022644)
XLA Ops:
  0.0 1.4 %fusion.13 = s32[]{:T(128)} fusion(s32[8]{0:T(128)} %param.9, s32[]{:T(128)S(6)} %axis_index.15), kind=kLoop, calls=%fused_computation.55 | loop fusion | flops 23 | bytes 40 | tf_op jit(solution)/shard_map/reduce_sum | solution.py:51
  3.4 0.7 broadcast_add_fusion
  4.1 0.1 slice_bitcast_fusion.5
  4.2 1.4 %fusion.15 = (s32[]{:T(128)}, s32[]{:T(128)}) fusion(s32[8]{0:T(128)} %param.9, s32[]{:T(128)S(6)} %select_n.127, s32[]{:T(128)S(6)} %select_n.124), kind=kLoop, calls=%fused_computation.57 | loop fusion | flops 46 | bytes 48 | tf_op jit(solution)/shard_map/reduce_sum | solution.py:55
  5.5 1.2 %iota_compare_fusion = (pred[8]{0:T(512)(128)(4,1)S(1)}, pred[8]{0:T(512)(128)(4,1)S(1)}) fusion(s32[]{:T(128)} %get-tuple-element.5, s32[]{:T(128)} %get-tuple-element.6), kind=kLoop, calls=%fused_computation.62 | loop fusion | flops 16 | bytes 24 | tf_op jit(solution)/shard_map/eq | solution.py:63
  6.8 0.7 fusion.8
  7.4 6.4 %all-to-all-start.1 = ((s32[8,1,16]{2,1,0:T(1,128)}), s32[8,1,16]{2,1,0:T(1,128)S(1)}, u32[]{:S(2)}, u32[]{:S(2)}) async-start(s32[8,1,16]{2,1,0:T(1,128)} %fusion.8), calls=%async_computation.1 | async-start | bytes 8192 | tf_op jit(solution)/shard_map/all_to_all | solution.py:78
  13.8 0.7 fusion.19
  14.5 0.8 %slice_bitcast_fusion.1 = (f32[16,512]{1,0:T(8,128)S(1)}, f32[16,512]{1,0:T(8,128)S(1)}, f32[16,512]{1,0:T(8,128)S(1)}, f32[16,512]{1,0:T(8,128)S(1)}) fusion(f32[1,64,512]{2,1,0:T(8,128)} %param.7, f32[1,64,512]{2,1,0:T(8,128)} %param.6), kind=kLoop, calls=%fused_computation.25 | loop fusion | bytes 262144 | tf_op jit(solution)/shard_map/jit(_where)/broadcast_in_dim | solution.py:67
  15.3 0.9 %select_add_fusion = (f32[8,16,512]{2,1,0:T(8,128)}, f32[8,16,512]{2,1,0:T(8,128)}) fusion(f32[16,512]{1,0:T(8,128)S(1)} %get-tuple-element.12, f32[16,512]{1,0:T(8,128)S(1)} %get-tuple-element.11, pred[8]{0:T(512)(128)(4,1)S(1)} %get-tuple-element.25, pred[8]{0:T(512)(128)(4,1)S(1)} %get-tuple-element.26, f32[16,512]{1,0:T(8,128)S(1)} %get-tuple-element.27, ...), kind=kLoop, calls=%fused_computation.18 | loop fusion | flops 393216 | bytes 655376 | tf_op jit(solution)/shard_map/add | solution.py:67
  20.0 1.3 %dynamic-slice.2 = u32[1]{0:T(128)} dynamic-slice(u32[32]{0:T(128)} %constant.145, u32[]{:T(128)S(6)} %add.195), dynamic_slice_sizes={1} | dynamic-slice | bytes 12
  21.9 5.1 %all-to-all-start = ((f32[8,16,512]{2,1,0:T(8,128)}), f32[8,16,512]{2,1,0:T(8,128)S(1)}, u32[]{:S(2)}, u32[]{:S(2)}) async-start(f32[8,16,512]{2,1,0:T(8,128)} %get-tuple-element.20), calls=%async_computation | async-start | bytes 524288 | tf_op jit(solution)/shard_map/all_to_all | solution.py:72
  27.1 0.2 add_dynamic-update-slice_fusion
  27.2 7.4 %all-reduce = s32[384]{0:T(512)S(1)} all-reduce(s32[384]{0:T(512)S(1)} %add_dynamic-update-slice_fusion), channel_id=1, replica_groups=mesh['region'=8,'state'=4] {'state'}, use_global_device_ids=true, to_apply=%add | all-reduce | flops 384 | bytes 3072
  34.6 0.8 %select_multiply_fusion = f32[256,384]{0,1:T(8,128)S(1)} fusion(s32[384]{0:T(512)S(1)} %get-tuple-element.18, s32[256]{0:T(256)S(1)} %get-tuple-element.23, s32[384]{0:T(512)S(1)} %get-tuple-element.17, s32[256]{0:T(256)S(1)} %get-tuple-element.24), kind=kLoop, calls=%fused_computation.12 | loop fusion | flops 4718592 | bytes 398336 | tf_op jit(solution)/shard_map/div | solution.py:41
  35.4 0.3 mul.120
  35.7 0.0 copy-start.1
  35.7 1.5 %copy.8 = f32[48,8,4,256]{3,1,2,0:T(8,128)} copy(f32[48,8,4,256]{3,2,1,0:T(4,128)S(1)} %bitcast.48) | data formatting | bytes 3145728
  37.2 5.1 %all-to-all-start.2 = ((f32[8,16,512]{2,1,0:T(8,128)}), f32[8,16,512]{2,1,0:T(8,128)S(1)}, u32[]{:S(2)}, u32[]{:S(2)}) async-start(f32[8,16,512]{2,1,0:T(8,128)} %get-tuple-element.19), calls=%async_computation.2 | async-start | bytes 524288 | tf_op jit(solution)/shard_map/all_to_all | solution.py:75
  42.3 12.7 %all_gather.9 = f32[384,512]{1,0:T(8,128)S(1)} all-gather(f32[96,512]{1,0:T(8,128)S(1)} %pad_maximum_fusion), channel_id=1, replica_groups=mesh['region'=8,'state'=4] {'state'}, dimensions={0}, use_global_device_ids=true | all-gather | bytes 983040 | tf_op jit(solution)/shard_map/all_gather | solution.py:106
  55.0 5.3 %bitcast_multiply_fusion = f32[1024,384]{0,1:T(8,128)} fusion(f32[1024,384]{0,1:T(8,128)} %bitcast.47, f32[384,512]{1,0:T(8,128)S(1)} %all_gather.9, f32[1024,512]{1,0:T(8,128)S(1)} %bitcast.45), kind=kOutput, calls=%fused_computation.1 | convolution fusion | flops 2416312320 | bytes 6029312 | tf_op jit(solution)/shard_map/rm,pm->rp/dot_general | solution.py:38
  60.4 3.1 %copy.7 = f32[1024,384]{1,0:T(8,128)} copy(f32[1024,384]{0,1:T(8,128)} %bitcast_multiply_fusion) | data formatting | bytes 3145728 | tf_op jit(solution)/shard_map/reshape.79
  63.5 10.1 %all_gather.11 = f32[384,512]{1,0:T(8,128)S(1)} all-gather(f32[96,512]{1,0:T(8,128)S(1)} %pad_maximum_fusion.1), channel_id=1, replica_groups=mesh['region'=8,'state'=4] {'state'}, dimensions={0}, use_global_device_ids=true | all-gather | bytes 983040 | tf_op jit(solution)/shard_map/all_gather | solution.py:107
  73.6 6.2 %convolution_bitcast_fusion = f32[1,4,256,512]{3,2,1,0:T(8,128)} fusion(f32[4,256,384]{2,1,0:T(8,128)} %bitcast.46, f32[384,512]{1,0:T(8,128)S(1)} %all_gather.11), kind=kOutput, calls=%fused_computation | convolution fusion | flops 2415919104 | bytes 4456448 | tf_op jit(solution)/shard_map/dot_general | solution.py:43
  (16 shorter events, 0.1 us)
Async XLA Ops:
  0.0 55.0 %copy-start = (f32[1,4,256,512]{3,2,1,0:T(8,128)S(1)}, f32[1,4,256,512]{3,2,1,0:T(8,128)}, u32[]{:S(2)}) copy-start(f32[1,4,256,512]{3,2,1,0:T(8,128)} %param.5) | copy-start | bytes 6291460
  7.4 14.5 %all-to-all-start.1 = ((s32[8,1,16]{2,1,0:T(1,128)}), s32[8,1,16]{2,1,0:T(1,128)S(1)}, u32[]{:S(2)}, u32[]{:S(2)}) async-start(s32[8,1,16]{2,1,0:T(1,128)} %fusion.8), calls=%async_computation.1 | async-start | bytes 8192 | tf_op jit(solution)/shard_map/all_to_all | solution.py:78
  21.9 15.3 %all-to-all-start = ((f32[8,16,512]{2,1,0:T(8,128)}), f32[8,16,512]{2,1,0:T(8,128)S(1)}, u32[]{:S(2)}, u32[]{:S(2)}) async-start(f32[8,16,512]{2,1,0:T(8,128)} %get-tuple-element.20), calls=%async_computation | async-start | bytes 524288 | tf_op jit(solution)/shard_map/all_to_all | solution.py:72
  35.7 6.6 %copy-start.1 = (f32[1,64,512]{2,1,0:T(8,128)S(1)}, f32[1,64,512]{2,1,0:T(8,128)}, u32[]{:S(2)}) copy-start(f32[1,64,512]{2,1,0:T(8,128)} %param.6) | copy-start | bytes 393220
  37.2 26.2 %all-to-all-start.2 = ((f32[8,16,512]{2,1,0:T(8,128)}), f32[8,16,512]{2,1,0:T(8,128)S(1)}, u32[]{:S(2)}, u32[]{:S(2)}) async-start(f32[8,16,512]{2,1,0:T(8,128)} %get-tuple-element.19), calls=%async_computation.2 | async-start | bytes 524288 | tf_op jit(solution)/shard_map/all_to_all | solution.py:75
  60.4 3.1 %copy-start.2 = (f32[1,64,512]{2,1,0:T(8,128)S(1)}, f32[1,64,512]{2,1,0:T(8,128)}, u32[]{:S(2)}) copy-start(f32[1,64,512]{2,1,0:T(8,128)} %param.7) | copy-start | bytes 393220
where the time goes:
time: 80.5 us; the launch traced here: 79.8 us
  blocking collectives  30.2 us (38%)
  starting transfers between devices  16.5 us (20%)
  matrix products  11.5 us (14%)
  other arithmetic  8.01 us (10%)
  local copies, waits for them, and re-layouts  7.03 us (9%)
  between operations  6.46 us (8%)
    all_gather x1, blocking collectives, on_device(): lax.all_gather(joined[0], 'state', axis=0, tiled=True)  12.7 us
    all_gather x1, blocking collectives, on_device(): lax.all_gather(joined[1], 'state', axis=0, tiled=True)  10.1 us
    unnamed x1, blocking collectives  7.37 us
    all_to_all x1, starting transfers between devices, on_device(): lax.all_to_all(place(low_set[2], high_set[2]), 'region', split_axis=0, co...  6.35 us
    dot_general x1, matrix products, add_block(): return jnp.dot(covar, piece_weight, precision=lax.Precision.HIGHEST)  6.17 us
    dot_general x1, matrix products, add_block(): jnp.einsum('rm,pm->rp', flat_state, piece_anom, precision=lax.Precision.H...  5.33 us
    all_to_all x1, starting transfers between devices, on_device(): lax.all_to_all(place(low_set[0], high_set[0]), 'region', split_axis=0, co...  5.11 us
    all_to_all x1, starting transfers between devices, on_device(): lax.all_to_all(place(low_set[1], high_set[1]), 'region', split_axis=0, co...  5.08 us
  transfers between devices with their start and end apart: 3, of which 0 were waited for; matrix products, arithmetic and copies ran while one was open for 19% of the time, Pallas kernels for 0%

commit v1 on v0

v1 whole, which is shorter than its diff:
```python
import functools

import jax
import jax.numpy as jnp
from jax import lax
from jax.experimental import pallas as pl
from jax.experimental.pallas import tpu as pltpu
from jax.sharding import PartitionSpec as P

SECT_W = 32
LAT = 8
HALF = 4
CAP = 16
COLS = 256
EDGE = 2 * HALF * LAT
SUB = 8
LANES = 128
VMEM = pl.BlockSpec(memory_space=pltpu.VMEM)
SMEM = pl.BlockSpec(memory_space=pltpu.SMEM)
ANY = pl.BlockSpec(memory_space=pl.ANY)


def partner(index, step, size):
    return index ^ step if size & (size - 1) == 0 else (index + size - step) % size


def target(index, step, size):
    return index ^ step if size & (size - 1) == 0 else (index + step) % size


def exchange(value, axis, step):
    size = lax.axis_size(axis)
    return lax.ppermute(value, axis, [(i, target(i, step, size)) for i in range(size)])


def gaspari(scaled):
    inside = scaled * scaled * (scaled * (scaled * (0.5 - 0.25 * scaled) + 0.625) - 5.0 / 3.0) + 1.0
    floored = jnp.maximum(scaled, 1.0)
    outside = (
        scaled * (scaled * (scaled * (scaled * (scaled / 12.0 - 0.5) + 0.625) + 5.0 / 3.0) - 5.0)
        + 4.0
        - 2.0 / (3.0 * floored)
    )
    return jnp.where(scaled <= 1.0, inside, jnp.where(scaled < 2.0, outside, 0.0))


def taper(first_col, rows, cells, lon_shift):
    cols = first_col + lax.broadcasted_iota(jnp.int32, (rows, cells.shape[1]), 0)
    obs = cells.astype(jnp.int32)
    lon_gap = cols // LAT - (obs // LAT + lon_shift)
    lat_gap = cols % LAT - obs % LAT
    scaled = jnp.sqrt((lon_gap * lon_gap + lat_gap * lat_gap).astype(jnp.float32)) / HALF
    return gaspari(scaled)


def split(value):
    high = value.astype(jnp.bfloat16)
    return high, (value - high.astype(jnp.float32)).astype(jnp.bfloat16)


def product(left, right, dims):
    dot = functools.partial(lax.dot_general, dimension_numbers=(dims, ((), ())), preferred_element_type=jnp.float32)
    return dot(left[0], right[0]) + (dot(left[0], right[1]) + dot(left[1], right[0]))


NT = ((1,), (1,))
NN = ((1,), (0,))


def folded(rows):
    return jnp.concatenate([rows[i : i + SUB] for i in range(0, rows.shape[0], SUB)], axis=1)


def unfolded(tiles, members):
    return jnp.concatenate([tiles[:, i : i + members] for i in range(0, tiles.shape[1], members)], axis=0)


def pack_kernel(sector_ref, anom_ref, weight_ref, cell_ref, own_ref, *slot_refs):
    regions = lax.axis_size("region")
    me = lax.axis_index("region")
    count = weight_ref.shape[0]
    members = weight_ref.shape[1]
    mine = sector_ref[me]
    left, right = jnp.int32(0), jnp.int32(0)
    for q in range(regions):
        sector = sector_ref[q]
        left = jnp.where(sector == lax.rem(mine + regions - 1, regions), q, left)
        right = jnp.where(sector == lax.rem(mine + 1, regions), q, right)
    cells = jnp.broadcast_to(cell_ref[...].astype(jnp.float32), (SUB, count)).astype(jnp.bfloat16)
    entry = lax.broadcasted_iota(jnp.int32, (count, LANES), 0)
    lane = lax.broadcasted_iota(jnp.int32, (count, LANES), 1)

    def spread(start, width):
        pick = jnp.where(entry == start + lane % width, 1.0, 0.0).astype(jnp.bfloat16)
        return lax.dot_general(cells, pick, (NN, ((), ())), preferred_element_type=jnp.float32)

    own_ref[:, : count // SUB * members] = folded(weight_ref[...])
    own_ref[:, count // SUB * members :] = spread(0, count)
    low = (folded(anom_ref[:CAP, :]), folded(weight_ref[:CAP, :]), spread(0, CAP))
    high = (folded(anom_ref[count - CAP :, :]), folded(weight_ref[count - CAP :, :]), spread(count - CAP, CAP))
    wide = CAP // SUB * members
    for step, slot in enumerate(slot_refs, start=1):
        to_right = target(me, step, regions) == right
        for (start, stop), lo, hi in zip(((0, wide), (wide, 2 * wide), (2 * wide, 2 * wide + LANES)), low, high):
            slot[:, start:stop] = jnp.where(to_right, hi, lo)


def pick_kernel(sector_ref, *refs):
    *slot_refs, halo_ref = refs
    regions = lax.axis_size("region")
    me = lax.axis_index("region")
    mine = sector_ref[me]
    width = slot_refs[0].shape[1]
    for step, slot in enumerate(slot_refs, start=1):
        sector = sector_ref[partner(me, step, regions)]

        @pl.when(sector == lax.rem(mine + regions - 1, regions))
        def _():
            halo_ref[:, :width] = slot[...]

        @pl.when(sector == lax.rem(mine + 1, regions))
        def _():
            halo_ref[:, width:] = slot[...]


def own_kernel(blocks, state_ref, *refs):
    anom_refs, pack_refs, (out_ref, a_hi, a_lo, w_hi, w_lo, rho_ref) = refs[:blocks], refs[blocks : 2 * blocks], refs[2 * blocks :]
    count, members = anom_refs[0].shape
    rows = state_ref.shape[0]

    @pl.when(pl.program_id(0) == 0)
    def _():
        lane = lax.broadcasted_iota(jnp.int32, (1, LANES), 1)
        tiles = [pack[:1, count // SUB * members :] for pack in pack_refs]
        for b in range(blocks):
            here = pl.ds(b * count, count)
            a_hi[here, :], a_lo[here, :] = split(anom_refs[b][...])
            w_hi[here, :], w_lo[here, :] = split(unfolded(pack_refs[b][:, : count // SUB * members], members))
        each = LANES // count
        for g in range(0, blocks, each):
            cells = tiles[g]
            for b in range(1, each):
                cells = jnp.where(lane >= b * count, tiles[g + b], cells)
            rho_ref[:, g * count : g * count + LANES] = taper(0, rows, cells, 0) / (members - 1)

    covar = product(split(state_ref[...]), (a_hi[...], a_lo[...]), NT) * rho_ref[...]
    out_ref[...] = product(split(covar), (w_hi[...], w_lo[...]), NN)


def halo_kernel(blocks, total_ref, state_ref, *refs):
    halo_refs, (out_ref, total_buf, state_buf, in_sem, state_sem, out_sem) = refs[:blocks], refs[blocks:]
    levels, columns, members = state_ref.shape
    wide = CAP // SUB * members
    width = halo_refs[0].shape[1] // 2
    starts = (0, columns - EDGE)
    loads = [
        (
            pltpu.make_async_copy(total_ref.at[l, pl.ds(c, EDGE)], total_buf.at[s, pl.ds(l * EDGE, EDGE)], in_sem.at[s, l]),
            pltpu.make_async_copy(state_ref.at[l, pl.ds(c, EDGE)], state_buf.at[s, pl.ds(l * EDGE, EDGE)], state_sem.at[s, l]),
        )
        for s, c in enumerate(starts)
        for l in range(levels)
    ]
    for total_load, state_load in loads:
        state_load.start()
        total_load.start()
    lane = lax.broadcasted_iota(jnp.int32, (1, LANES), 1)
    per = LANES // CAP
    parts = []
    for s, shift in enumerate((-SECT_W, SECT_W)):
        at = s * width
        anom = split(jnp.concatenate([unfolded(h[:, at : at + wide], members) for h in halo_refs], axis=0))
        weight = split(jnp.concatenate([unfolded(h[:, at + wide : at + 2 * wide], members) for h in halo_refs], axis=0))
        tiles = [h[:1, at + 2 * wide : at + width] for h in halo_refs]
        groups = []
        for g in range(0, blocks, per):
            cells = tiles[g]
            for b in range(1, min(per, blocks - g)):
                cells = jnp.where(lane >= b * CAP, tiles[g + b], cells)
            groups.append(cells)
        cells = jnp.concatenate(groups, axis=1)[:, : blocks * CAP]
        parts.append((anom, weight, taper(starts[s], EDGE, cells, shift) / (members - 1)))
    for _, state_load in loads:
        state_load.wait()
    deltas = []
    for s, (anom, weight, rho) in enumerate(parts):
        covar = product(split(state_buf[s]), anom, NT)
        covar = (covar.reshape(levels, EDGE, -1) * rho[None]).reshape(levels * EDGE, -1)
        deltas.append(product(split(covar), weight, NN))
    stores = []
    for s, c in enumerate(starts):
        for l in range(levels):
            loads[s * levels + l][0].wait()
        total_buf[s] += deltas[s]
        for l in range(levels):
            stores.append(
                pltpu.make_async_copy(total_buf.at[s, pl.ds(l * EDGE, EDGE)], out_ref.at[l, pl.ds(c, EDGE)], out_sem.at[s, l])
            )
            stores[-1].start()
    for store in stores:
        store.wait()


def on_device(state_anom, obs_anom, obs_weight, obs_cell, sector_of):
    f32 = jnp.float32
    regions, owners = lax.axis_size("region"), lax.axis_size("state")
    levels, columns, members = state_anom.shape[1:]
    own_anom, own_weight = obs_anom[0], obs_weight[0]
    count = own_anom.shape[0]
    blocks = owners

    anoms = [own_anom] + [exchange(own_anom, "state", k) for k in range(1, owners)]

    slot = jax.ShapeDtypeStruct((SUB, 2 * (CAP // SUB) * members + LANES), f32)
    own_pack, *slots = pl.pallas_call(
        pack_kernel,
        out_shape=[jax.ShapeDtypeStruct((SUB, count // SUB * members + LANES), f32)] + [slot] * (regions - 1),
        in_specs=[SMEM, VMEM, VMEM, VMEM],
        out_specs=[VMEM] * regions,
        name="pack",
    )(sector_of, own_anom, own_weight, obs_cell)
    got = [exchange(slots[k - 1], "region", k) for k in range(1, regions)]
    packs = [own_pack] + [exchange(own_pack, "state", k) for k in range(1, owners)]
    halo = pl.pallas_call(
        pick_kernel,
        out_shape=jax.ShapeDtypeStruct((SUB, 2 * slot.shape[1]), f32),
        in_specs=[SMEM] + [VMEM] * (regions - 1),
        out_specs=VMEM,
        name="pick",
    )(sector_of, *got)
    halos = [halo] + [exchange(halo, "state", k) for k in range(1, owners)]

    obs = blocks * count
    whole = lambda a: pl.BlockSpec(a.shape, lambda l: (0,) * a.ndim)
    level = pl.BlockSpec((None, columns, members), lambda l: (l, 0, 0))
    state = state_anom[0]
    bf16 = jnp.bfloat16
    total = pl.pallas_call(
        functools.partial(own_kernel, blocks),
        out_shape=jax.ShapeDtypeStruct(state.shape, f32),
        grid=(levels,),
        in_specs=[level] + [whole(a) for a in anoms + packs],
        out_specs=level,
        scratch_shapes=[pltpu.VMEM((obs, members), bf16)] * 4 + [pltpu.VMEM((columns, obs), f32)],
        cost_estimate=pl.CostEstimate(
            flops=12 * levels * columns * obs * members, bytes_accessed=8 * state.size + 8 * obs * members, transcendentals=0
        ),
        name="own",
    )(state, *anoms, *packs)
    out = pl.pallas_call(
        functools.partial(halo_kernel, blocks),
        out_shape=jax.ShapeDtypeStruct(state.shape, f32),
        in_specs=[ANY, ANY] + [VMEM] * blocks,
        out_specs=ANY,
        scratch_shapes=[pltpu.VMEM((2, levels * EDGE, members), f32)] * 2 + [pltpu.SemaphoreType.DMA((2, levels))] * 3,
        input_output_aliases={0: 0},
        name="halo",
    )(total, state, *halos)
    return out[None]


def solution(mesh):
    in_specs = (
        P("region", "state", None, None),
        P("region", "state", None),
        P("region", "state", None),
        P("region", "state"),
        P(),
    )
    out_specs = P("region", "state", None, None)
    return jax.shard_map(on_device, mesh=mesh, in_specs=in_specs, out_specs=out_specs, check_vma=False)
```

time: 80.5 us -> 48.4 us (0.60)
  blocking collectives: 30.2 us -> 0 us
  Pallas kernels: 0 us -> 16.7 us
  matrix products: 11.5 us -> 0 us
  waiting for transfers between devices: 0.01 us -> 8.94 us
  other arithmetic: 8.01 us -> 0 us
  between operations: 6.46 us -> 0.14 us
  local copies, waits for them, and re-layouts: 7.03 us -> 2.01 us
  starting transfers between devices: 16.5 us -> 20.1 us
    all_gather x2 -> x0, blocking collectives: 22.9 us -> none  [the longest x1 12.7 us: on_device(): lax.all_gather(joined[0], 'state', axis=0, tiled=True)]
    ppermute x0 -> x16, starting transfers between devices: none -> 20.1 us  [exchange(): lax.ppermute(value, axis, [(i, target(i, step, size)) for i in range(size)])]
    pallas_call x0 -> x4, Pallas kernels: none -> 16.7 us  [the longest x1 7.12 us: on_device(): pl.pallas_call(functools.partial(own_kernel, blocks), out_shape=jax.Shape...]
    all_to_all x3 -> x0, starting transfers between devices: 16.5 us -> none  [the longest x1 6.35 us: on_device(): lax.all_to_all(place(low_set[2], high_set[2]), 'region', split_axis=0, co...]
    dot_general x2 -> x0, matrix products: 11.5 us -> none  [the longest x1 6.17 us: add_block(): return jnp.dot(covar, piece_weight, precision=lax.Precision.HIGHEST)]
    ppermute x0 -> x16, waiting for transfers between devices: none -> 8.94 us  [exchange(): lax.ppermute(value, axis, [(i, target(i, step, size)) for i in range(size)])]
    unnamed x1 -> x0, blocking collectives: 7.37 us -> none
    another operation x1 -> x0, local copies, waits for them, and re-layouts: 3.06 us -> none
  transfers between devices with their start and end apart: 3 -> 16, of which waited for: 0 -> 3; matrix products, arithmetic and copies ran while one was open for 19% -> 0% of each run, Pallas kernels for 0% -> 19%
where the time goes in v1:
time: 48.4 us; the launch traced here: 47.9 us
  starting transfers between devices  20.1 us (42%)
  Pallas kernels  16.7 us (35%)
  waiting for transfers between devices  8.94 us (18%)
  local copies, waits for them, and re-layouts  2.01 us (4%)
    ppermute x16, starting transfers between devices, exchange(): lax.ppermute(value, axis, [(i, target(i, step, size)) for i in range(size)])  20.1 us
    ppermute x16, waiting for transfers between devices, exchange(): lax.ppermute(value, axis, [(i, target(i, step, size)) for i in range(size)])  8.94 us
    pallas_call x1, Pallas kernels, on_device(): pl.pallas_call(functools.partial(own_kernel, blocks), out_shape=jax.Shape...  7.12 us
    pallas_call x1, Pallas kernels, on_device(): pl.pallas_call(functools.partial(halo_kernel, blocks), out_shape=jax.Shap...  5.75 us
    unnamed x32, local copies, waits for them, and re-layouts  2.01 us
    pallas_call x1, Pallas kernels, on_device(): pl.pallas_call(pack_kernel, out_shape=[jax.ShapeDtypeStruct((SUB, count /...  1.92 us
    pallas_call x1, Pallas kernels, on_device(): pl.pallas_call(pick_kernel, out_shape=jax.ShapeDtypeStruct((SUB, 2 * slot...  1.86 us
  transfers between devices with their start and end apart: 16, of which 3 were waited for; matrix products, arithmetic and copies ran while one was open for 0% of the time, Pallas kernels for 19%

profile of v1, /device:TPU:0, one launch (start us, length us, event | category | flops | bytes accessed | tf_op | source)
XLA Modules:
  0.0 47.9 jit_solution(2596622357873801467)
XLA Ops:
  0.0 1.9 %pack.1 = (f32[8,4224]{1,0:T(8,128)}, f32[8,2176]{1,0:T(8,128)}, f32[8,2176]{1,0:T(8,128)}, f32[8,2176]{1,0:T(8,128)}, f32[8,2176]{1,0:T(8,128)}, /*index=5*/f32...) custom-call(s32[8]{0:T(128)} %sector_ref.3, f32[64,512]{1,0:T(8,128)} %bitcast.7, f32[64,512]{1,0:T(8,128)} %bitcast.6, ...), custom_call_target="tpu_custom_call" | custom-call | tf_op jit(solution)/shard_map/pack/pallas_call | solution.py:215
  1.9 0.5 %collective-permute-start.6 = (f32[8,2176]{1,0:T(8,128)}, f32[8,2176]{1,0:T(8,128)S(1)}, u32[]{:S(2)}, u32[]{:S(2)}) collective-permute-start(f32[8,2176]{1,0:T(8,128)} %get-tuple-element.14), channel_id=1, source_target_pairs={{0,4},{4,0},{8,12},{12,8},{16,20},{20,16},{24,28},{28,24},{1,5},{5... | collective-permute-start | bytes 208904 | tf_op jit(solution)/shard_map/ppermute | solution.py:33
  2.4 2.6 %collective-permute-start.7 = (f32[8,2176]{1,0:T(8,128)}, f32[8,2176]{1,0:T(8,128)S(1)}, u32[]{:S(2)}, u32[]{:S(2)}) collective-permute-start(f32[8,2176]{1,0:T(8,128)} %get-tuple-element.15), channel_id=1, source_target_pairs={{0,8},{4,12},{8,0},{12,4},{16,24},{20,28},{24,16},{28,20},{1,9},{5... | collective-permute-start | bytes 208904 | tf_op jit(solution)/shard_map/ppermute | solution.py:33
  5.1 2.6 %collective-permute-start.2 = (f32[64,512]{1,0:T(8,128)}, f32[64,512]{1,0:T(8,128)S(1)}, u32[]{:S(2)}, u32[]{:S(2)}) collective-permute-start(f32[64,512]{1,0:T(8,128)} %bitcast.8), channel_id=1, source_target_pairs={{0,3},{1,2},{2,1},{3,0},{4,7},{5,6},{6,5},{7,4},{8,11},{9,10},{10,... | collective-permute-start | bytes 393224 | tf_op jit(solution)/shard_map/ppermute | solution.py:33
  7.7 2.6 %collective-permute-start.9 = (f32[8,2176]{1,0:T(8,128)}, f32[8,2176]{1,0:T(8,128)S(1)}, u32[]{:S(2)}, u32[]{:S(2)}) collective-permute-start(f32[8,2176]{1,0:T(8,128)} %get-tuple-element.17), channel_id=1, source_target_pairs={{0,16},{4,20},{8,24},{12,28},{16,0},{20,4},{24,8},{28,12},{1,17},{... | collective-permute-start | bytes 208904 | tf_op jit(solution)/shard_map/ppermute | solution.py:33
  10.3 3.3 %collective-permute-start.11 = (f32[8,2176]{1,0:T(8,128)}, f32[8,2176]{1,0:T(8,128)S(1)}, u32[]{:S(2)}, u32[]{:S(2)}) collective-permute-start(f32[8,2176]{1,0:T(8,128)} %get-tuple-element.19), channel_id=1, source_target_pairs={{0,24},{4,28},{8,16},{12,20},{16,8},{20,12},{24,0},{28,4},{1,25},{... | collective-permute-start | bytes 208904 | tf_op jit(solution)/shard_map/ppermute | solution.py:33
  13.6 0.4 collective-permute-start.12
  14.1 0.8 %collective-permute-done.9.refs_3_ = f32[8,2176]{1,0:T(8,128)S(1)} collective-permute-done((f32[8,2176]{1,0:T(8,128)}, f32[8,2176]{1,0:T(8,128)S(1)}, u32[]{:S(2)}, u32[]{:S(2)}) %collective-permute-start.9) | collective-permute-done | bytes 69664 | tf_op jit(solution)/shard_map/ppermute | solution.py:33
  14.8 0.5 %collective-permute-start.5 = (f32[8,4224]{1,0:T(8,128)}, f32[8,4224]{1,0:T(8,128)S(1)}, u32[]{:S(2)}, u32[]{:S(2)}) collective-permute-start(f32[8,4224]{1,0:T(8,128)} %get-tuple-element.13.refs_4_), channel_id=1, source_target_pairs={{0,3},{1,2},{2,1},{3,0},{4,7},{5,6},{6,5},{7,4},{8,11},{9,10},{10,... | collective-permute-start | bytes 405512 | tf_op jit(solution)/shard_map/ppermute | solution.py:33
  15.3 5.1 %collective-permute-done.10.refs_4_ = f32[8,2176]{1,0:T(8,128)S(1)} collective-permute-done((f32[8,2176]{1,0:T(8,128)}, f32[8,2176]{1,0:T(8,128)S(1)}, u32[]{:S(2)}, u32[]{:S(2)}) %collective-permute-start.10) | collective-permute-done | bytes 69664 | tf_op jit(solution)/shard_map/ppermute | solution.py:33
  20.4 0.5 %collective-permute-start.4 = (f32[8,4224]{1,0:T(8,128)}, f32[8,4224]{1,0:T(8,128)S(1)}, u32[]{:S(2)}, u32[]{:S(2)}) collective-permute-start(f32[8,4224]{1,0:T(8,128)} %get-tuple-element.13.refs_4_), channel_id=1, source_target_pairs={{0,2},{1,3},{2,0},{3,1},{4,6},{5,7},{6,4},{7,5},{8,10},{9,11},{10,... | collective-permute-start | bytes 405512 | tf_op jit(solution)/shard_map/ppermute | solution.py:33
  20.9 1.3 %collective-permute-start.3 = (f32[8,4224]{1,0:T(8,128)}, f32[8,4224]{1,0:T(8,128)S(1)}, u32[]{:S(2)}, u32[]{:S(2)}) collective-permute-start(f32[8,4224]{1,0:T(8,128)} %get-tuple-element.13.refs_4_), channel_id=1, source_target_pairs={{0,1},{1,0},{2,3},{3,2},{4,5},{5,4},{6,7},{7,6},{8,9},{9,8},{10,11... | collective-permute-start | bytes 405512 | tf_op jit(solution)/shard_map/ppermute | solution.py:33
  22.2 0.7 %collective-permute-start.1 = (f32[64,512]{1,0:T(8,128)}, f32[64,512]{1,0:T(8,128)S(1)}, u32[]{:S(2)}, u32[]{:S(2)}) collective-permute-start(f32[64,512]{1,0:T(8,128)} %bitcast.9), channel_id=1, source_target_pairs={{0,2},{1,3},{2,0},{3,1},{4,6},{5,7},{6,4},{7,5},{8,10},{9,11},{10,... | collective-permute-start | bytes 393224 | tf_op jit(solution)/shard_map/ppermute | solution.py:33
  23.0 1.5 %collective-permute-start = (f32[64,512]{1,0:T(8,128)}, f32[64,512]{1,0:T(8,128)S(1)}, u32[]{:S(2)}, u32[]{:S(2)}) collective-permute-start(f32[64,512]{1,0:T(8,128)} %bitcast.10), channel_id=1, source_target_pairs={{0,1},{1,0},{2,3},{3,2},{4,5},{5,4},{6,7},{7,6},{8,9},{9,8},{10,11... | collective-permute-start | bytes 393224 | tf_op jit(solution)/shard_map/ppermute | solution.py:33
  24.5 1.9 %pick.1.refs_0_ = f32[8,4352]{1,0:T(8,128)} custom-call(s32[8]{0:T(128)} %sector_ref.3, f32[8,2176]{1,0:T(8,128)} %copy-done.3, f32[8,2176]{1,0:T(8,128)} %copy-done.4, f32[8,2176]{1,0:T(8,128)} %copy-done.5, f32[8,2176]{1,0:T(8,128)} %copy-done.6, f32[8,2176]{1,0:T(8,128)} %copy-done.7, f32[8,2176]{1,0:T(8,128)} %copy-done.8, f32[8,2176]{1,0:T(8,128)} %copy-done.9), custom_call_target="tpu_custom_call" | custom-call | tf_op jit(solution)/shard_map/pick/pallas_call | solution.py:224
  26.3 3.1 %collective-permute-done.1.refs_2_ = f32[64,512]{1,0:T(8,128)S(1)} collective-permute-done((f32[64,512]{1,0:T(8,128)}, f32[64,512]{1,0:T(8,128)S(1)}, u32[]{:S(2)}, u32[]{:S(2)}) %collective-permute-start.1) | collective-permute-done | bytes 131104 | tf_op jit(solution)/shard_map/ppermute | solution.py:33
  29.4 0.8 %collective-permute-start.15 = (f32[8,4352]{1,0:T(8,128)}, f32[8,4352]{1,0:T(8,128)S(1)}, u32[]{:S(2)}, u32[]{:S(2)}) collective-permute-start(f32[8,4352]{1,0:T(8,128)} %pick.1.refs_0_), channel_id=1, source_target_pairs={{0,3},{1,2},{2,1},{3,0},{4,7},{5,6},{6,5},{7,4},{8,11},{9,10},{10,... | collective-permute-start | bytes 417800 | tf_op jit(solution)/shard_map/ppermute | solution.py:33
  30.3 1.2 %collective-permute-start.14 = (f32[8,4352]{1,0:T(8,128)}, f32[8,4352]{1,0:T(8,128)S(1)}, u32[]{:S(2)}, u32[]{:S(2)}) collective-permute-start(f32[8,4352]{1,0:T(8,128)} %pick.1.refs_0_), channel_id=1, source_target_pairs={{0,2},{1,3},{2,0},{3,1},{4,6},{5,7},{6,4},{7,5},{8,10},{9,11},{10,... | collective-permute-start | bytes 417800 | tf_op jit(solution)/shard_map/ppermute | solution.py:33
  31.4 1.5 %collective-permute-start.13 = (f32[8,4352]{1,0:T(8,128)}, f32[8,4352]{1,0:T(8,128)S(1)}, u32[]{:S(2)}, u32[]{:S(2)}) collective-permute-start(f32[8,4352]{1,0:T(8,128)} %pick.1.refs_0_), channel_id=1, source_target_pairs={{0,1},{1,0},{2,3},{3,2},{4,5},{5,4},{6,7},{7,6},{8,9},{9,8},{10,11... | collective-permute-start | bytes 417800 | tf_op jit(solution)/shard_map/ppermute | solution.py:33
  33.0 0.6 %copy-done.11 = f32[8,4224]{1,0:T(8,128)} copy-done((f32[8,4224]{1,0:T(8,128)}, f32[8,4224]{1,0:T(8,128)S(1)}, u32[]{:S(2)}) %copy-start.11) | copy-done | bytes 135192
  33.6 7.1 %own.1.total_ref = f32[4,256,512]{2,1,0:T(8,128)} custom-call(f32[4,256,512]{2,1,0:T(8,128)} %bitcast.4, f32[64,512]{1,0:T(8,128)} %bitcast.11, f32[64,512]{1,0:T(8,128)} %copy-done.15, f32[64,512]{1,0:T(8,128)} %copy-done.14, f32[64,512]{1,0:T(8,128)} %copy-done.13, f32[8,4224]{1,0:T(8,128)} %get-tuple-element.13.refs_4_, f32[8,4224]{1,0:T(8,128)} %copy-done.12, ...), custom_call_target="tpu_custom_call" | custom-call | flops 1610612736 | bytes 5242880 | tf_op jit(solution)/shard_map/own/pallas_call | solution.py:238
  40.8 0.6 %copy-done = f32[8,4352]{1,0:T(8,128)} copy-done((f32[8,4352]{1,0:T(8,128)}, f32[8,4352]{1,0:T(8,128)S(1)}, u32[]{:S(2)}) %copy-start) | copy-done | bytes 139288
  41.5 0.6 %copy-done.2 = f32[8,4352]{1,0:T(8,128)} copy-done((f32[8,4352]{1,0:T(8,128)}, f32[8,4352]{1,0:T(8,128)S(1)}, u32[]{:S(2)}) %copy-start.2) | copy-done | bytes 139288
  42.1 5.7 %halo.1 = f32[4,256,512]{2,1,0:T(8,128)} custom-call(f32[4,256,512]{2,1,0:T(8,128)} %own.1.total_ref, f32[4,256,512]{2,1,0:T(8,128)} %bitcast.5, f32[8,4352]{1,0:T(8,128)} %pick.1.refs_0_, f32[8,4352]{1,0:T(8,128)} %copy-done.2, f32[8,4352]{1,0:T(8,128)} %copy-done.1, f32[8,4352]{1,0:T(8,128)} %copy-done), custom_call_target="tpu_custom_call", output_to_operand_aliasing={{}: (0, {})} | custom-call | tf_op jit(solution)/shard_map/halo/pallas_call | solution.py:250
  (44 shorter events, 0.2 us)
Async XLA Ops:
  1.9 8.4 %collective-permute-start.6 = (f32[8,2176]{1,0:T(8,128)}, f32[8,2176]{1,0:T(8,128)S(1)}, u32[]{:S(2)}, u32[]{:S(2)}) collective-permute-start(f32[8,2176]{1,0:T(8,128)} %get-tuple-element.14), channel_id=1, source_target_pairs={{0,4},{4,0},{8,12},{12,8},{16,20},{20,16},{24,28},{28,24},{1,5},{5... | collective-permute-start | bytes 208904 | tf_op jit(solution)/shard_map/ppermute | solution.py:33
  2.4 7.9 %collective-permute-start.7 = (f32[8,2176]{1,0:T(8,128)}, f32[8,2176]{1,0:T(8,128)S(1)}, u32[]{:S(2)}, u32[]{:S(2)}) collective-permute-start(f32[8,2176]{1,0:T(8,128)} %get-tuple-element.15), channel_id=1, source_target_pairs={{0,8},{4,12},{8,0},{12,4},{16,24},{20,28},{24,16},{28,20},{1,9},{5... | collective-permute-start | bytes 208904 | tf_op jit(solution)/shard_map/ppermute | solution.py:33
  5.0 8.6 %collective-permute-start.8 = (f32[8,2176]{1,0:T(8,128)}, f32[8,2176]{1,0:T(8,128)S(1)}, u32[]{:S(2)}, u32[]{:S(2)}) collective-permute-start(f32[8,2176]{1,0:T(8,128)} %get-tuple-element.16), channel_id=1, source_target_pairs={{0,12},{4,8},{8,4},{12,0},{16,28},{20,24},{24,20},{28,16},{1,13},{... | collective-permute-start | bytes 208904 | tf_op jit(solution)/shard_map/ppermute | solution.py:33
  5.1 17.9 %collective-permute-start.2 = (f32[64,512]{1,0:T(8,128)}, f32[64,512]{1,0:T(8,128)S(1)}, u32[]{:S(2)}, u32[]{:S(2)}) collective-permute-start(f32[64,512]{1,0:T(8,128)} %bitcast.8), channel_id=1, source_target_pairs={{0,3},{1,2},{2,1},{3,0},{4,7},{5,6},{6,5},{7,4},{8,11},{9,10},{10,... | collective-permute-start | bytes 393224 | tf_op jit(solution)/shard_map/ppermute | solution.py:33
  7.7 7.1 %collective-permute-start.9 = (f32[8,2176]{1,0:T(8,128)}, f32[8,2176]{1,0:T(8,128)S(1)}, u32[]{:S(2)}, u32[]{:S(2)}) collective-permute-start(f32[8,2176]{1,0:T(8,128)} %get-tuple-element.17), channel_id=1, source_target_pairs={{0,16},{4,20},{8,24},{12,28},{16,0},{20,4},{24,8},{28,12},{1,17},{... | collective-permute-start | bytes 208904 | tf_op jit(solution)/shard_map/ppermute | solution.py:33
  10.3 14.1 %copy-start.3 = (f32[8,2176]{1,0:T(8,128)}, f32[8,2176]{1,0:T(8,128)S(1)}, u32[]{:S(2)}) copy-start(f32[8,2176]{1,0:T(8,128)S(1)} %collective-permute-done.6.refs_0_) | copy-start | bytes 208900
  10.3 10.1 %collective-permute-start.10 = (f32[8,2176]{1,0:T(8,128)}, f32[8,2176]{1,0:T(8,128)S(1)}, u32[]{:S(2)}, u32[]{:S(2)}) collective-permute-start(f32[8,2176]{1,0:T(8,128)} %get-tuple-element.18), channel_id=1, source_target_pairs={{0,20},{4,16},{8,28},{12,24},{16,4},{20,0},{24,12},{28,8},{1,21},{... | collective-permute-start | bytes 208904 | tf_op jit(solution)/shard_map/ppermute | solution.py:33
  10.3 14.1 %copy-start.4 = (f32[8,2176]{1,0:T(8,128)}, f32[8,2176]{1,0:T(8,128)S(1)}, u32[]{:S(2)}) copy-start(f32[8,2176]{1,0:T(8,128)S(1)} %collective-permute-done.7.refs_1_) | copy-start | bytes 208900
  10.3 10.6 %collective-permute-start.11 = (f32[8,2176]{1,0:T(8,128)}, f32[8,2176]{1,0:T(8,128)S(1)}, u32[]{:S(2)}, u32[]{:S(2)}) collective-permute-start(f32[8,2176]{1,0:T(8,128)} %get-tuple-element.19), channel_id=1, source_target_pairs={{0,24},{4,28},{8,16},{12,20},{16,8},{20,12},{24,0},{28,4},{1,25},{... | collective-permute-start | bytes 208904 | tf_op jit(solution)/shard_map/ppermute | solution.py:33
  13.6 10.8 %copy-start.5 = (f32[8,2176]{1,0:T(8,128)}, f32[8,2176]{1,0:T(8,128)S(1)}, u32[]{:S(2)}) copy-start(f32[8,2176]{1,0:T(8,128)S(1)} %collective-permute-done.8.refs_2_) | copy-start | bytes 208900
  13.6 8.6 %collective-permute-start.12 = (f32[8,2176]{1,0:T(8,128)}, f32[8,2176]{1,0:T(8,128)S(1)}, u32[]{:S(2)}, u32[]{:S(2)}) collective-permute-start(f32[8,2176]{1,0:T(8,128)} %get-tuple-element.20), channel_id=1, source_target_pairs={{0,28},{4,24},{8,20},{12,16},{16,12},{20,8},{24,4},{28,0},{1,29},{... | collective-permute-start | bytes 208904 | tf_op jit(solution)/shard_map/ppermute | solution.py:33
  14.8 9.6 %copy-start.6 = (f32[8,2176]{1,0:T(8,128)}, f32[8,2176]{1,0:T(8,128)S(1)}, u32[]{:S(2)}) copy-start(f32[8,2176]{1,0:T(8,128)S(1)} %collective-permute-done.9.refs_3_) | copy-start | bytes 208900
  14.8 16.6 %collective-permute-start.5 = (f32[8,4224]{1,0:T(8,128)}, f32[8,4224]{1,0:T(8,128)S(1)}, u32[]{:S(2)}, u32[]{:S(2)}) collective-permute-start(f32[8,4224]{1,0:T(8,128)} %get-tuple-element.13.refs_4_), channel_id=1, source_target_pairs={{0,3},{1,2},{2,1},{3,0},{4,7},{5,6},{6,5},{7,4},{8,11},{9,10},{10,... | collective-permute-start | bytes 405512 | tf_op jit(solution)/shard_map/ppermute | solution.py:33
  20.4 4.1 %copy-start.7 = (f32[8,2176]{1,0:T(8,128)}, f32[8,2176]{1,0:T(8,128)S(1)}, u32[]{:S(2)}) copy-start(f32[8,2176]{1,0:T(8,128)S(1)} %collective-permute-done.10.refs_4_) | copy-start | bytes 208900
  20.4 12.6 %collective-permute-start.4 = (f32[8,4224]{1,0:T(8,128)}, f32[8,4224]{1,0:T(8,128)S(1)}, u32[]{:S(2)}, u32[]{:S(2)}) collective-permute-start(f32[8,4224]{1,0:T(8,128)} %get-tuple-element.13.refs_4_), channel_id=1, source_target_pairs={{0,2},{1,3},{2,0},{3,1},{4,6},{5,7},{6,4},{7,5},{8,10},{9,11},{10,... | collective-permute-start | bytes 405512 | tf_op jit(solution)/shard_map/ppermute | solution.py:33
  20.9 3.6 %copy-start.8 = (f32[8,2176]{1,0:T(8,128)}, f32[8,2176]{1,0:T(8,128)S(1)}, u32[]{:S(2)}) copy-start(f32[8,2176]{1,0:T(8,128)S(1)} %collective-permute-done.11.refs_5_) | copy-start | bytes 208900
  20.9 12.1 %collective-permute-start.3 = (f32[8,4224]{1,0:T(8,128)}, f32[8,4224]{1,0:T(8,128)S(1)}, u32[]{:S(2)}, u32[]{:S(2)}) collective-permute-start(f32[8,4224]{1,0:T(8,128)} %get-tuple-element.13.refs_4_), channel_id=1, source_target_pairs={{0,1},{1,0},{2,3},{3,2},{4,5},{5,4},{6,7},{7,6},{8,9},{9,8},{10,11... | collective-permute-start | bytes 405512 | tf_op jit(solution)/shard_map/ppermute | solution.py:33
  22.2 7.2 %collective-permute-start.1 = (f32[64,512]{1,0:T(8,128)}, f32[64,512]{1,0:T(8,128)S(1)}, u32[]{:S(2)}, u32[]{:S(2)}) collective-permute-start(f32[64,512]{1,0:T(8,128)} %bitcast.9), channel_id=1, source_target_pairs={{0,2},{1,3},{2,0},{3,1},{4,6},{5,7},{6,4},{7,5},{8,10},{9,11},{10,... | collective-permute-start | bytes 393224 | tf_op jit(solution)/shard_map/ppermute | solution.py:33
  23.0 10.0 %copy-start.13 = (f32[64,512]{1,0:T(8,128)}, f32[64,512]{1,0:T(8,128)S(1)}, u32[]{:S(2)}) copy-start(f32[64,512]{1,0:T(8,128)S(1)} %collective-permute-done.2.refs_3_) | copy-start | bytes 393220
  23.0 7.3 %collective-permute-start = (f32[64,512]{1,0:T(8,128)}, f32[64,512]{1,0:T(8,128)S(1)}, u32[]{:S(2)}, u32[]{:S(2)}) collective-permute-start(f32[64,512]{1,0:T(8,128)} %bitcast.10), channel_id=1, source_target_pairs={{0,1},{1,0},{2,3},{3,2},{4,5},{5,4},{6,7},{7,6},{8,9},{9,8},{10,11... | collective-permute-start | bytes 393224 | tf_op jit(solution)/shard_map/ppermute | solution.py:33
  29.4 3.5 %copy-start.14 = (f32[64,512]{1,0:T(8,128)}, f32[64,512]{1,0:T(8,128)S(1)}, u32[]{:S(2)}) copy-start(f32[64,512]{1,0:T(8,128)S(1)} %collective-permute-done.1.refs_2_) | copy-start | bytes 393220
  29.4 11.3 %collective-permute-start.15 = (f32[8,4352]{1,0:T(8,128)}, f32[8,4352]{1,0:T(8,128)S(1)}, u32[]{:S(2)}, u32[]{:S(2)}) collective-permute-start(f32[8,4352]{1,0:T(8,128)} %pick.1.refs_0_), channel_id=1, source_target_pairs={{0,3},{1,2},{2,1},{3,0},{4,7},{5,6},{6,5},{7,4},{8,11},{9,10},{10,... | collective-permute-start | bytes 417800 | tf_op jit(solution)/shard_map/ppermute | solution.py:33
  30.3 10.5 %collective-permute-start.14 = (f32[8,4352]{1,0:T(8,128)}, f32[8,4352]{1,0:T(8,128)S(1)}, u32[]{:S(2)}, u32[]{:S(2)}) collective-permute-start(f32[8,4352]{1,0:T(8,128)} %pick.1.refs_0_), channel_id=1, source_target_pairs={{0,2},{1,3},{2,0},{3,1},{4,6},{5,7},{6,4},{7,5},{8,10},{9,11},{10,... | collective-permute-start | bytes 417800 | tf_op jit(solution)/shard_map/ppermute | solution.py:33
  31.4 9.4 %collective-permute-start.13 = (f32[8,4352]{1,0:T(8,128)}, f32[8,4352]{1,0:T(8,128)S(1)}, u32[]{:S(2)}, u32[]{:S(2)}) collective-permute-start(f32[8,4352]{1,0:T(8,128)} %pick.1.refs_0_), channel_id=1, source_target_pairs={{0,1},{1,0},{2,3},{3,2},{4,5},{5,4},{6,7},{7,6},{8,9},{9,8},{10,11... | collective-permute-start | bytes 417800 | tf_op jit(solution)/shard_map/ppermute | solution.py:33
  (8 other events, 9.8 us)
